TPU v7x, 32 devices: a whole 2x2x4 slice. The times are simulated.
32 devices in a mesh: seqa: 4 (over x, core), seqb: 8 (over z, y).
Axes of the slice: x: 2, y: 2, z: 4, core: 2. Of those that a mesh axis runs over, the one named last changes fastest.
Arguments:
- sequence_input: bfloat16 [16384, 640], P(('seqa', 'seqb')), may hold values from -6 to 6
- w_prev: bfloat16 [3, 640, 1280], P(None, 'seqa'), may hold values from -0.15625 to 0.15625
- w_now: bfloat16 [3, 640, 1280], P(None, 'seqa'), may hold values from -0.15625 to 0.15625
- conv_bias: float32 [3, 1280], replicated, may hold values from -4 to 4
- w_mix: bfloat16 [3, 640, 640], P(None, None, 'seqa'), may hold values from -0.25 to 0.25
Outputs:
- seq_out: bfloat16 [16384, 640], P(('seqa', 'seqb'))
All inputs are finite; a program needn't handle non-finite values.
Results may differ from a plain program's by a relative error of at most 0.0052.
Values may be sent and summed in bfloat16 or wider, within the bound.
A program may use at most 64 MiB of HBM per device.

v0:
```python
import functools

import jax
import jax.numpy as jnp
from jax import lax
from jax.experimental import pallas as pl
from jax.experimental.pallas import tpu as pltpu
from jax.sharding import PartitionSpec as P

DILATIONS = (128, 512, 2048)
EPS = 1e-06
TILE = 16
GROUP = 4
MESH_ID = pl.DeviceIdType.MESH


def from_behind(value, axis, by):
    peers = lax.axis_size(axis)
    pairs = [(i, i + by) for i in range(peers) if 0 <= i + by < peers]
    return lax.ppermute(value, axis, pairs)


def norm_rows(values):
    scale = lax.rsqrt(jnp.mean(values * values, axis=1, keepdims=True) + EPS)
    return (values * scale).astype(jnp.bfloat16)


def block_prior(normed, dilation_step):
    rows = normed.shape[0]
    whole = dilation_step // rows
    part = dilation_step % rows
    pieces = []
    if part > 0:
        pieces.append(from_behind(normed[rows - part :], ("seqa", "seqb"), whole + 1))
    head = normed[: rows - part]
    if whole > 0:
        head = from_behind(head, ("seqa", "seqb"), whole)
    pieces.append(head)
    return jnp.concatenate(pieces, axis=0)


def one_layer(hidden_state, tap_prev, tap_now, bias, mixing, dilation_step):
    normed = norm_rows(hidden_state)
    earlier = block_prior(normed, dilation_step)
    dim = hidden_state.shape[1]
    pre = bias[None, :] + jnp.dot(
        earlier,
        lax.all_gather(tap_prev, "seqa", axis=0, tiled=True),
        preferred_element_type=jnp.float32,
    )
    pre = pre + jnp.dot(
        normed,
        lax.all_gather(tap_now, "seqa", axis=0, tiled=True),
        preferred_element_type=jnp.float32,
    )
    hidden = (pre[:, :dim] * jax.nn.sigmoid(pre[:, dim:])).astype(jnp.bfloat16)
    return hidden_state + jnp.dot(
        hidden,
        lax.all_gather(mixing, "seqa", axis=1, tiled=True),
        preferred_element_type=jnp.float32,
    )


def plain_local(sequence_input, w_prev, w_now, conv_bias, w_mix):
    state = sequence_input.astype(jnp.float32)
    for layer, step in enumerate(DILATIONS):
        state = one_layer(
            state, w_prev[layer], w_now[layer], conv_bias[layer], w_mix[layer], step
        )
    return state.astype(jnp.bfloat16)


def flip(value, bit):
    return value + bit - 2 * bit * ((value // bit) % 2)


def block_kernel(
    na, nb, chunk,
    x_hbm, wp_hbm, wn_hbm, bias_ref, wm_hbm,
    out_ref,
    w, xin, xs, state, u0, u1, u2, h1, h2, pre, osend, oin,
    load_sem, x_sem, own_sem, send, recv, halo_send, halo_recv,
):
    layers, dim = wp_hbm.shape[0], x_hbm.shape[1]
    wide = 2 * dim
    shard = wp_hbm.shape[1]
    rows = x_hbm.shape[0]
    n = na * nb
    part = DILATIONS[0]
    a, b = lax.axis_index("seqa"), lax.axis_index("seqb")
    me = a * nb + b
    a1, a2 = flip(a, 1), flip(a, 2)
    b1, b2 = flip(b, 1), flip(b, 2)
    p = b % GROUP
    p1, p2 = flip(p, 1), flip(p, 2)
    p3 = flip(p1, 2)
    big = 2 * TILE
    direct = GROUP * big

    def at(index):
        return (index // nb, index % nb)

    hop = DILATIONS[2] // rows
    half, q = b // hop, b % hop
    other = 1 - half
    pair = (a, (b + hop) % nb)
    follow_a, follow_q = (a + 1) % na, (q + 1) % hop
    wrap = (q + 1) // hop
    next_b = half * hop + follow_q

    loads = []
    for l in range(layers):
        loads.append([
            pltpu.make_async_copy(wp_hbm.at[l], w.at[l, a, :, pl.ds(0, wide)], load_sem.at[l, 0]),
            pltpu.make_async_copy(wn_hbm.at[l], w.at[l, a, :, pl.ds(wide, wide)], load_sem.at[l, 1]),
            pltpu.make_async_copy(wm_hbm.at[l], w.at[l, a, :, pl.ds(2 * wide, dim)], load_sem.at[l, 2]),
        ])
    for c in loads[0]:
        c.start()
    x_load = pltpu.make_async_copy(x_hbm, xin, x_sem)
    x_load.start()
    barrier = pltpu.get_barrier_semaphore()
    near = [(a1, b), (a2, b), (a, b1), (a, b2)]
    near += [pair, at((me + 1) % n), at((me + n - 1) % n)]
    near += [at((me + hop - 1) % n), at((me + n - hop + 1) % n)]
    near += [(follow_a, b), ((a + na - 1) % na, b)]
    near += [(a, next_b), (follow_a, next_b)]
    last_b = half * hop + (q + hop - 1) % hop
    near += [(a, last_b), ((a + na - 1) % na, last_b)]
    for dev in near:
        pl.semaphore_signal(barrier, inc=1, device_id=dev, device_id_type=MESH_ID)
    pl.semaphore_wait(barrier, len(near))

    def move(l, k, owner, start, size, dev):
        ref = w.at[l, owner, pl.ds(pl.multiple_of(start, TILE), size)]
        return pltpu.make_async_remote_copy(
            src_ref=ref, dst_ref=ref, send_sem=send.at[l, k], recv_sem=recv.at[l, k],
            device_id=dev, device_id_type=MESH_ID,
        )

    core, across, ynear, znear = (a1, b), (a2, b), (a, b1), (a, b2)
    moves = []
    for l in range(layers):
        moves.append([
            move(l, 0, a, p * big, TILE, across),
            move(l, 1, a, p * big + TILE, TILE, across),
            move(l, 2, a, direct, shard - direct, across),
            move(l, 3, a, 0, shard, core),
            move(l, 4, a2, p * big, TILE, ynear),
            move(l, 5, a2, p * big, TILE, znear),
            move(l, 6, a2, p * big + TILE, TILE, ynear),
            move(l, 7, a2, p * big + TILE, TILE, znear),
            move(l, 8, a2, p * big, big, core),
            move(l, 9, a2, direct, shard - direct, core),
            move(l, 10, a2, p1 * big, TILE, znear),
            move(l, 11, a2, p1 * big, big, core),
            move(l, 12, a2, p2 * big + TILE, TILE, ynear),
            move(l, 13, a2, p2 * big, big, core),
            move(l, 14, a2, p3 * big, TILE, core),
            move(l, 15, a2, p3 * big + TILE, TILE, core),
        ])

    def after(l, k, then):
        moves[l][k].wait_recv()
        for t in then:
            moves[l][t].start()

    def forward_first(l):
        after(l, 0, (4, 5))
        after(l, 1, (6, 7, 8))

    def forward_second(l):
        after(l, 4, (10,))
        after(l, 5, ())
        after(l, 7, (12, 13))
        after(l, 6, (11,))

    def forward_last(l):
        after(l, 10, (14,))
        after(l, 12, (15,))

    def forward_direct(l):
        after(l, 2, (9,))

    def finish(l):
        for k in (3, 8, 9, 11, 13, 14, 15):
            after(l, k, ())

    def halo(src, dst, slot, dev):
        return pltpu.make_async_remote_copy(
            src_ref=src, dst_ref=dst, send_sem=halo_send.at[slot], recv_sem=halo_recv.at[slot],
            device_id=dev, device_id_type=MESH_ID,
        )

    pair_low = halo(xin.at[pl.ds(part, rows - part)], xs.at[0], 0, pair)
    pair_high = halo(xin.at[pl.ds(0, chunk)], xs.at[1, pl.ds(part, chunk)], 0, pair)
    tail_src = xin.at[pl.ds(rows - part, part)]
    tail_next = halo(tail_src, xs.at[0, pl.ds(0, part)], 1, at((me + 1) % n))
    tail_back = halo(tail_src, xs.at[1, pl.ds(0, part)], 2, at((me + n - hop + 1) % n))
    sends_next = jnp.logical_and(me + 1 < n, (b + 1) % nb < hop)
    sends_back = jnp.logical_and(b >= hop - 1, b < 2 * hop - 1)
    takes_next = jnp.logical_and(half == 0, me > 0)

    def second(s):
        to = s + wrap
        slot = to % 2
        dev = ((a + to // 2) % na, next_b)
        return pltpu.make_async_remote_copy(
            src_ref=u1.at[s], dst_ref=h1.at[slot], send_sem=halo_send.at[3 + slot],
            recv_sem=halo_recv.at[3 + slot], device_id=dev, device_id_type=MESH_ID,
        ), a + to // 2 < na

    third = halo(u2.at[1], h2.at[0], 5, (follow_a, b))
    back = halo(osend, oin, 6, pair)

    def send_pair():
        @pl.when(half == 0)
        def _():
            pair_low.start()

        @pl.when(half == 1)
        def _():
            pair_high.start()

    near_cut = (b // 2) % 2 != half
    own_low = pltpu.make_async_copy(xin.at[pl.ds(0, chunk)], xs.at[0, pl.ds(part, chunk)], own_sem)
    own_high = pltpu.make_async_copy(xin.at[pl.ds(part, rows - part)], xs.at[1], own_sem)

    for c in loads[0]:
        c.wait()
    moves[0][0].start()
    moves[0][1].start()
    for c in loads[1]:
        c.start()
    x_load.wait()

    @pl.when(sends_next)
    def _():
        tail_next.start()

    @pl.when(sends_back)
    def _():
        tail_back.start()

    pl.when(near_cut)(send_pair)

    @pl.when(half == 0)
    def _():
        own_low.start()
        own_low.wait()

    @pl.when(half == 1)
    def _():
        own_high.start()
        own_high.wait()

    for c in loads[1]:
        c.wait()
    for c in loads[2]:
        c.start()
    moves[1][0].start()
    moves[1][1].start()
    moves[0][2].start()
    moves[0][3].start()
    for c in loads[2]:
        c.wait()
    moves[1][2].start()
    moves[1][3].start()
    for k in (0, 1, 2, 3):
        moves[2][k].start()

    @pl.when(me == 0)
    def _():
        xs[0, pl.ds(0, part), :] = jnp.zeros((part, dim), xs.dtype)

    @pl.when(jnp.logical_and(a == 0, q == 0))
    def _():
        h1[0] = jnp.zeros(h1.shape[1:], h1.dtype)

    @pl.when(a == 0)
    def _():
        h2[0] = jnp.zeros(h2.shape[1:], h2.dtype)

    def enter(s):
        block = xs[s].astype(jnp.float32)
        u0[s] = norm_rows(block)
        state[s] = block[part:]

    forward_first(0)

    @pl.when(takes_next)
    def _():
        tail_next.wait_recv()

    enter(half)
    forward_second(0)
    pl.when(jnp.logical_not(near_cut))(send_pair)
    forward_first(1)
    forward_last(0)
    forward_direct(0)
    finish(0)

    def tap(l, lo):
        return w[l, :, :, lo : lo + wide].reshape(na * shard, wide)

    def now_part(l, now, s):
        pre[s] = bias_ref[l : l + 1, :] + jnp.dot(
            now, tap(l, wide), preferred_element_type=jnp.float32
        )

    def rest_part(l, earlier, s):
        total = pre[s] + jnp.dot(earlier, tap(l, 0), preferred_element_type=jnp.float32)
        hidden = (total[:, :dim] * jax.nn.sigmoid(total[:, dim:])).astype(jnp.bfloat16)
        mix = w[l, :, :, 2 * wide :].reshape(na * shard, dim)
        return state[s] + lax.dot_general(
            hidden, mix, (((1,), (1,)), ((), ())), preferred_element_type=jnp.float32
        )

    for c, s in enumerate((half, other)):
        if c == 1:
            @pl.when(half == 1)
            def _():
                pair_low.wait_recv()

            @pl.when(half == 0)
            def _():
                pair_high.wait_recv()
                tail_back.wait_recv()

            enter(s)
        now_part(0, u0[s, pl.ds(part, chunk), :], s)
        if c == 1:
            forward_first(2)
        new = rest_part(0, u0[s, pl.ds(0, chunk), :], s)
        state[s] = new
        u1[s] = norm_rows(new)
        copy, there = second(s)
        pl.when(there)(copy.start)
        if c == 0:
            forward_second(1)
    forward_last(1)
    forward_direct(1)
    finish(1)
    for s in (half, other):
        now_part(1, u1[s], s)
    forward_second(2)
    for c, s in enumerate((half, other)):
        @pl.when(jnp.logical_or(me % nb % hop + s > 0, a > 0))
        def _(s=s):
            halo(u1.at[s], h1.at[s], 3 + s, pair).wait_recv()

        new = rest_part(1, h1[s], s)
        state[s] = new
        normed = norm_rows(new)
        u2[s] = normed

        @pl.when(s == 0)
        def _(normed=normed):
            h2[1] = normed

        @pl.when(jnp.logical_and(s == 1, a + 1 < na))
        def _():
            third.start()

    forward_last(2)
    forward_direct(2)
    finish(2)
    for c, s in enumerate((other, half)):
        now_part(2, u2[s], s)

        @pl.when(jnp.logical_and(s == 0, a > 0))
        def _():
            third.wait_recv()

        new = rest_part(2, h2[s], s).astype(out_ref.dtype)
        if c == 0:
            osend[...] = new
            back.start()
        else:
            out_ref[pl.ds(pl.multiple_of(half * chunk, chunk), chunk), :] = new
    back.wait_recv()
    out_ref[pl.ds(pl.multiple_of(other * chunk, chunk), chunk), :] = oin[...]

    for l in range(layers):
        for m in moves[l]:
            m.wait_send()
    back.wait_send()
    for s in range(2):
        copy, there = second(s)
        pl.when(there)(copy.wait_send)
    pl.when(a + 1 < na)(third.wait_send)
    pl.when(sends_next)(tail_next.wait_send)
    pl.when(sends_back)(tail_back.wait_send)
    pl.when(half == 0)(pair_low.wait_send)
    pl.when(half == 1)(pair_high.wait_send)


def kernel_local(na, nb, sequence_input, w_prev, w_now, conv_bias, w_mix):
    rows, dim = sequence_input.shape
    layers, shard, wide = w_prev.shape
    chunk = rows // 2
    part = DILATIONS[0]
    bf16, f32 = jnp.bfloat16, jnp.float32
    halos = 7
    anywhere = pl.BlockSpec(memory_space=pl.ANY)
    vmem = pl.BlockSpec(memory_space=pltpu.VMEM)
    return pl.pallas_call(
        functools.partial(block_kernel, na, nb, chunk),
        out_shape=jax.ShapeDtypeStruct((rows, dim), bf16),
        in_specs=[anywhere, anywhere, anywhere, vmem, anywhere],
        out_specs=vmem,
        scratch_shapes=[
            pltpu.VMEM((layers, na, shard, 2 * wide + dim), bf16),
            pltpu.VMEM((rows, dim), bf16),
            pltpu.VMEM((2, part + chunk, dim), bf16),
            pltpu.VMEM((2, chunk, dim), f32),
            pltpu.VMEM((2, part + chunk, dim), bf16),
            pltpu.VMEM((2, chunk, dim), bf16),
            pltpu.VMEM((2, chunk, dim), bf16),
            pltpu.VMEM((2, chunk, dim), bf16),
            pltpu.VMEM((2, chunk, dim), bf16),
            pltpu.VMEM((2, chunk, wide), f32),
            pltpu.VMEM((chunk, dim), bf16),
            pltpu.VMEM((chunk, dim), bf16),
            pltpu.SemaphoreType.DMA((layers, 3)),
            pltpu.SemaphoreType.DMA,
            pltpu.SemaphoreType.DMA,
            pltpu.SemaphoreType.DMA((layers, 16)),
            pltpu.SemaphoreType.DMA((layers, 16)),
            pltpu.SemaphoreType.DMA((halos,)),
            pltpu.SemaphoreType.DMA((halos,)),
        ],
        compiler_params=pltpu.CompilerParams(
            collective_id=0, has_side_effects=True, vmem_limit_bytes=56 * 2**20
        ),
    )(sequence_input, w_prev, w_now, conv_bias, jnp.swapaxes(w_mix, 1, 2))


def local(na, nb, sequence_input, w_prev, w_now, conv_bias, w_mix):
    rows = sequence_input.shape[0]
    shard = w_prev.shape[1]
    fits = (
        na == 4
        and nb % GROUP == 0
        and shard % TILE == 0
        and shard > GROUP * 2 * TILE
        and rows % (4 * TILE) == 0
        and rows == 4 * DILATIONS[0]
        and DILATIONS[1] == rows
        and 2 * DILATIONS[2] == nb * rows
    )
    body = functools.partial(kernel_local, na, nb) if fits else plain_local
    return body(sequence_input, w_prev, w_now, conv_bias, w_mix)


def solution(mesh):
    return jax.shard_map(
        functools.partial(local, mesh.shape["seqa"], mesh.shape["seqb"]),
        mesh=mesh,
        in_specs=(
            P(("seqa", "seqb"), None),
            P(None, "seqa", None),
            P(None, "seqa", None),
            P(),
            P(None, None, "seqa"),
        ),
        out_specs=P(("seqa", "seqb"), None),
        check_vma=False,
    )
```

profile of v0, /device:TPU:29, one launch (start us, length us, event | category | flops | bytes accessed | tf_op | source)
XLA Modules:
  0.0 79.9 jit_solution(3692938481691639278)
XLA Ops:
  0.0 77.9 %shard_map.55 = bf16[512,640]{1,0:T(8,128)(2,1)} custom-call(bf16[512,640]{1,0:T(8,128)(2,1)} %x_hbm.1, bf16[3,160,1280]{2,1,0:T(8,128)(2,1)} %wp_hbm.1, bf16[3,160,1280]{2,1,0:T(8,128)(2,1)} %wn_hbm.1, f32[3,1280]{1,0:T(4,128)} %bias_ref.1, bf16[3,160,640]{2,1,0:T(8,128)(2,1)} %bitcast.1), custom_call_target="tpu_custom_call" | custom-call | tf_op jit(solution)/shard_map/pallas_call | solution.py:407
  77.9 2.0 %copy.7 = bf16[512,640]{1,0:T(8,128)(2,1)} copy(bf16[512,640]{1,0:T(8,128)(2,1)} %shard_map.55) | data formatting | bytes 1310720
where the time goes:
time: 80.1 us; the launch traced here: 79.9 us
  Pallas kernels  77.9 us (97%)
  local copies, waits for them, and re-layouts  1.98 us (2%)
    pallas_call x1, Pallas kernels, kernel_local(): pl.pallas_call(functools.partial(block_kernel, na, nb, chunk), out_shape=...  77.9 us
    unnamed x1, local copies, waits for them, and re-layouts  1.98 us

commit v1 on v0

--- a/solution.py
+++ b/solution.py
@@ -79,7 +79,7 @@
     x_hbm, wp_hbm, wn_hbm, bias_ref, wm_hbm,
     out_ref,
     w, xin, xs, state, u0, u1, u2, h1, h2, pre, osend, oin,
-    load_sem, x_sem, own_sem, send, recv, halo_send, halo_recv,
+    load_sem, x_sem, own_sem, send, recv, halo_send, halo_recv, hello,
 ):
     layers, dim = wp_hbm.shape[0], x_hbm.shape[1]
     wide = 2 * dim
@@ -91,11 +91,11 @@
     me = a * nb + b
     a1, a2 = flip(a, 1), flip(a, 2)
     b1, b2 = flip(b, 1), flip(b, 2)
-    p = b % GROUP
-    p1, p2 = flip(p, 1), flip(p, 2)
-    p3 = flip(p1, 2)
-    big = 2 * TILE
-    direct = GROUP * big
+    tiles = shard // TILE
+    zs = tiles // 5
+    ys = tiles // 2 - zs
+    yb, zb = b % 2, b // 2 % 2
+    shares = [(ys, zs), (ys - 2, zs), (ys - 1, zs)]
 
     def at(index):
         return (index // nb, index % nb)
@@ -119,72 +119,100 @@
         c.start()
     x_load = pltpu.make_async_copy(x_hbm, xin, x_sem)
     x_load.start()
+    for l in range(1, layers):
+        for c in loads[l]:
+            c.start()
     barrier = pltpu.get_barrier_semaphore()
-    near = [(a1, b), (a2, b), (a, b1), (a, b2)]
-    near += [pair, at((me + 1) % n), at((me + n - 1) % n)]
-    near += [at((me + hop - 1) % n), at((me + n - hop + 1) % n)]
-    near += [(follow_a, b), ((a + na - 1) % na, b)]
-    near += [(a, next_b), (follow_a, next_b)]
+    first, last_one = b == 0, b == nb - 1
+    sends_next = jnp.logical_and(me + 1 < n, (b + 1) % nb < hop)
+    sends_back = jnp.logical_and(b >= hop - 1, b < 2 * hop - 1)
+    takes_next = jnp.logical_and(half == 0, me > 0)
+    z = b // 2
+    inner = jnp.logical_and(z > 0, z < nb // 2 - 1)
+    beside = (a, (b + nb - 2 + 4 * (z % 2)) % nb)
+
+    def greet(sem, more):
+        count = 4
+        for dev in ((a1, b), (a2, b), (a, b1), (a, b2)):
+            pl.semaphore_signal(sem, inc=1, device_id=dev, device_id_type=MESH_ID)
+        for to, dev, come in [(inner, beside, inner)] + more:
+            @pl.when(to)
+            def _(dev=dev):
+                pl.semaphore_signal(sem, inc=1, device_id=dev, device_id_type=MESH_ID)
+
+            count = count + come.astype(jnp.int32)
+        pl.semaphore_wait(sem, count)
+
+    up, down = a + 1 < na, a > 0
+    before = (a + na - 1) % na
     last_b = half * hop + (q + hop - 1) % hop
-    near += [(a, last_b), ((a + na - 1) % na, last_b)]
-    for dev in near:
-        pl.semaphore_signal(barrier, inc=1, device_id=dev, device_id_type=MESH_ID)
-    pl.semaphore_wait(barrier, len(near))
+    greet(barrier, [
+        (jnp.logical_and(first, down), (before, nb - 1), jnp.logical_and(last_one, up)),
+        (half == 0, (a, (b + hop - 1) % nb), sends_back),
+        (half == 0, pair, half == 1),
+        (q == 0, (a, last_b), wrap == 1),
+        (jnp.logical_and(q == 0, down), (before, last_b), jnp.logical_and(wrap == 1, up)),
+    ])
 
     def move(l, k, owner, start, size, dev):
-        ref = w.at[l, owner, pl.ds(pl.multiple_of(start, TILE), size)]
+        ref = w.at[l, owner, pl.ds(pl.multiple_of(start * TILE, TILE), size * TILE)]
         return pltpu.make_async_remote_copy(
             src_ref=ref, dst_ref=ref, send_sem=send.at[l, k], recv_sem=recv.at[l, k],
             device_id=dev, device_id_type=MESH_ID,
         )
 
     core, across, ynear, znear = (a1, b), (a2, b), (a, b1), (a, b2)
-    moves = []
-    for l in range(layers):
-        moves.append([
-            move(l, 0, a, p * big, TILE, across),
-            move(l, 1, a, p * big + TILE, TILE, across),
-            move(l, 2, a, direct, shard - direct, across),
-            move(l, 3, a, 0, shard, core),
-            move(l, 4, a2, p * big, TILE, ynear),
-            move(l, 5, a2, p * big, TILE, znear),
-            move(l, 6, a2, p * big + TILE, TILE, ynear),
-            move(l, 7, a2, p * big + TILE, TILE, znear),
-            move(l, 8, a2, p * big, big, core),
-            move(l, 9, a2, direct, shard - direct, core),
-            move(l, 10, a2, p1 * big, TILE, znear),
-            move(l, 11, a2, p1 * big, big, core),
-            move(l, 12, a2, p2 * big + TILE, TILE, ynear),
-            move(l, 13, a2, p2 * big, big, core),
-            move(l, 14, a2, p3 * big, TILE, core),
-            move(l, 15, a2, p3 * big + TILE, TILE, core),
-        ])
-
-    def after(l, k, then):
+    moves, orders, lasts = [], [], []
+    for l, (y, z) in enumerate(shares):
+        rest = tiles - 2 * (y + z)
+        own = (yb * y, 2 * y + zb * z, 2 * (y + z))
+        theirs = ((1 - yb) * y, 2 * y + (1 - zb) * z)
+        sizes = (y, z, rest)
+        order = [(1, i) for i in range(z)] + [(0, i) for i in range(y)] + [(2, i) for i in range(rest)]
+        pieces = len(order)
+        here = [move(l, k, a, own[f] + i, 1, across) for k, (f, i) in enumerate(order)]
+        relays = {}
+        for k, (f, i) in enumerate(order):
+            if f < 2:
+                relays[k] = len(here)
+                here.append(move(l, len(here), a2, own[f] + i, 1, (ynear, znear)[f]))
+        last = len(here)
+        here.append(move(l, last, a, 0, tiles, core))
+        for f in range(3):
+            if sizes[f]:
+                here.append(move(l, len(here), a2, own[f], sizes[f], core))
+        for f in range(2):
+            here.append(move(l, len(here), a2, theirs[f], sizes[f], core))
+        moves.append(here)
+        orders.append((order, sizes, relays))
+        lasts.append(last)
+
+    held = 0
+
+    def start_weights(l, hold=0):
+        for k in range(len(orders[l][0]) - hold):
+            moves[l][k].start()
+        moves[l][lasts[l]].start()
+
+    def relay(l, k):
+        order, sizes, relays = orders[l]
         moves[l][k].wait_recv()
-        for t in then:
-            moves[l][t].start()
-
-    def forward_first(l):
-        after(l, 0, (4, 5))
-        after(l, 1, (6, 7, 8))
-
-    def forward_second(l):
-        after(l, 4, (10,))
-        after(l, 5, ())
-        after(l, 7, (12, 13))
-        after(l, 6, (11,))
-
-    def forward_last(l):
-        after(l, 10, (14,))
-        after(l, 12, (15,))
-
-    def forward_direct(l):
-        after(l, 2, (9,))
+        f, i = order[k]
+        if k in relays:
+            moves[l][relays[k]].start()
+        if i == sizes[f] - 1:
+            moves[l][lasts[l] + 1 + f].start()
+
+    def gather(l, f):
+        order, sizes, relays = orders[l]
+        for k in relays:
+            if order[k][0] == f:
+                moves[l][relays[k]].wait_recv()
+        moves[l][len(moves[l]) - 2 + f].start()
 
     def finish(l):
-        for k in (3, 8, 9, 11, 13, 14, 15):
-            after(l, k, ())
+        for k in range(lasts[l], len(moves[l])):
+            moves[l][k].wait_recv()
 
     def halo(src, dst, slot, dev):
         return pltpu.make_async_remote_copy(
@@ -197,10 +225,6 @@
     tail_src = xin.at[pl.ds(rows - part, part)]
     tail_next = halo(tail_src, xs.at[0, pl.ds(0, part)], 1, at((me + 1) % n))
     tail_back = halo(tail_src, xs.at[1, pl.ds(0, part)], 2, at((me + n - hop + 1) % n))
-    sends_next = jnp.logical_and(me + 1 < n, (b + 1) % nb < hop)
-    sends_back = jnp.logical_and(b >= hop - 1, b < 2 * hop - 1)
-    takes_next = jnp.logical_and(half == 0, me > 0)
-
     def second(s):
         to = s + wrap
         slot = to % 2
@@ -228,12 +252,10 @@
 
     for c in loads[0]:
         c.wait()
-    moves[0][0].start()
-    moves[0][1].start()
-    for c in loads[1]:
-        c.start()
+    start_weights(0)
     x_load.wait()
 
+    greet(hello, [])
     @pl.when(sends_next)
     def _():
         tail_next.start()
@@ -254,21 +276,10 @@
         own_high.start()
         own_high.wait()
 
-    for c in loads[1]:
-        c.wait()
-    for c in loads[2]:
-        c.start()
-    moves[1][0].start()
-    moves[1][1].start()
-    moves[0][2].start()
-    moves[0][3].start()
-    for c in loads[2]:
-        c.wait()
-    moves[1][2].start()
-    moves[1][3].start()
-    for k in (0, 1, 2, 3):
-        moves[2][k].start()
-
+    for l in range(1, layers):
+        for c in loads[l]:
+            c.wait()
+        start_weights(l, held if l == layers - 1 else 0)
     @pl.when(me == 0)
     def _():
         xs[0, pl.ds(0, part), :] = jnp.zeros((part, dim), xs.dtype)
@@ -286,18 +297,21 @@
         u0[s] = norm_rows(block)
         state[s] = block[part:]
 
-    forward_first(0)
+    relay(0, 0)
+    relay(0, 1)
+    pl.when(jnp.logical_not(near_cut))(send_pair)
+    for k in range(2, 5):
+        relay(0, k)
+    gather(0, 1)
+    relay(1, 0)
+    gather(0, 0)
 
     @pl.when(takes_next)
     def _():
         tail_next.wait_recv()
 
     enter(half)
-    forward_second(0)
-    pl.when(jnp.logical_not(near_cut))(send_pair)
-    forward_first(1)
-    forward_last(0)
-    forward_direct(0)
+    relay(1, 1)
     finish(0)
 
     def tap(l, lo):
@@ -329,26 +343,25 @@
 
             enter(s)
         now_part(0, u0[s, pl.ds(part, chunk), :], s)
-        if c == 1:
-            forward_first(2)
+        relay(1, 2 + c)
         new = rest_part(0, u0[s, pl.ds(0, chunk), :], s)
         state[s] = new
         u1[s] = norm_rows(new)
         copy, there = second(s)
         pl.when(there)(copy.start)
-        if c == 0:
-            forward_second(1)
-    forward_last(1)
-    forward_direct(1)
+    for k in range(4, len(orders[1][0])):
+        relay(1, k)
+    gather(1, 1)
+    gather(1, 0)
     finish(1)
     for s in (half, other):
         now_part(1, u1[s], s)
-    forward_second(2)
     for c, s in enumerate((half, other)):
         @pl.when(jnp.logical_or(me % nb % hop + s > 0, a > 0))
         def _(s=s):
             halo(u1.at[s], h1.at[s], 3 + s, pair).wait_recv()
 
+        relay(2, c)
         new = rest_part(1, h1[s], s)
         state[s] = new
         normed = norm_rows(new)
@@ -362,8 +375,12 @@
         def _():
             third.start()
 
-    forward_last(2)
-    forward_direct(2)
+    for k in range(len(orders[2][0]) - held, len(orders[2][0])):
+        moves[2][k].start()
+    for k in range(2, len(orders[2][0])):
+        relay(2, k)
+    gather(2, 1)
+    gather(2, 0)
     finish(2)
     for c, s in enumerate((other, half)):
         now_part(2, u2[s], s)
@@ -402,6 +419,7 @@
     part = DILATIONS[0]
     bf16, f32 = jnp.bfloat16, jnp.float32
     halos = 7
+    copies = shard // TILE + 6
     anywhere = pl.BlockSpec(memory_space=pl.ANY)
     vmem = pl.BlockSpec(memory_space=pltpu.VMEM)
     return pl.pallas_call(
@@ -425,10 +443,11 @@
             pltpu.SemaphoreType.DMA((layers, 3)),
             pltpu.SemaphoreType.DMA,
             pltpu.SemaphoreType.DMA,
-            pltpu.SemaphoreType.DMA((layers, 16)),
-            pltpu.SemaphoreType.DMA((layers, 16)),
+            pltpu.SemaphoreType.DMA((layers, copies)),
+            pltpu.SemaphoreType.DMA((layers, copies)),
             pltpu.SemaphoreType.DMA((halos,)),
             pltpu.SemaphoreType.DMA((halos,)),
+            pltpu.SemaphoreType.REGULAR,
         ],
         compiler_params=pltpu.CompilerParams(
             collective_id=0, has_side_effects=True, vmem_limit_bytes=56 * 2**20
@@ -443,7 +462,8 @@
         na == 4
         and nb % GROUP == 0
         and shard % TILE == 0
-        and shard > GROUP * 2 * TILE
+        and shard % (2 * TILE) == 0
+        and shard >= 5 * TILE
         and rows % (4 * TILE) == 0
         and rows == 4 * DILATIONS[0]
         and DILATIONS[1] == rows

time: 80.1 us -> 73.2 us (0.914); the launches traced: 79.9 us -> 71.7 us
  Pallas kernels: 77.9 us -> 69.7 us
    pallas_call x1, Pallas kernels: 77.9 us -> 69.7 us  [kernel_local(): pl.pallas_call(functools.partial(block_kernel, na, nb, chunk), out_shape=...]
where the time goes in v1:
time: 73.2 us; the launch traced here: 71.7 us
  Pallas kernels  69.7 us (95%)
  local copies, waits for them, and re-layouts  1.98 us (3%)
    pallas_call x1, Pallas kernels, kernel_local(): pl.pallas_call(functools.partial(block_kernel, na, nb, chunk), out_shape=...  69.7 us
    unnamed x1, local copies, waits for them, and re-layouts  1.98 us

profile of v1, /device:TPU:29, one launch (start us, length us, event | category | flops | bytes accessed | tf_op | source)
XLA Modules:
  0.0 71.7 jit_solution(15022373968702599386)
XLA Ops:
  0.0 69.7 %shard_map.55 = bf16[512,640]{1,0:T(8,128)(2,1)} custom-call(bf16[512,640]{1,0:T(8,128)(2,1)} %x_hbm.1, bf16[3,160,1280]{2,1,0:T(8,128)(2,1)} %wp_hbm.1, bf16[3,160,1280]{2,1,0:T(8,128)(2,1)} %wn_hbm.1, f32[3,1280]{1,0:T(4,128)} %bias_ref.1, bf16[3,160,640]{2,1,0:T(8,128)(2,1)} %bitcast.1), custom_call_target="tpu_custom_call" | custom-call | tf_op jit(solution)/shard_map/pallas_call | solution.py:425
  69.7 2.0 %copy.7 = bf16[512,640]{1,0:T(8,128)(2,1)} copy(bf16[512,640]{1,0:T(8,128)(2,1)} %shard_map.55) | data formatting | bytes 1310720

commit v2 on v1

v2 whole, which is shorter than its diff:
```python
import functools

import jax
import jax.numpy as jnp
from jax import lax
from jax.experimental import pallas as pl
from jax.experimental.pallas import tpu as pltpu
from jax.sharding import PartitionSpec as P

DILATIONS = (128, 512, 2048)
EPS = 1e-06
TILE = 16
GROUP = 4
MESH_ID = pl.DeviceIdType.MESH


def from_behind(value, axis, by):
    peers = lax.axis_size(axis)
    pairs = [(i, i + by) for i in range(peers) if 0 <= i + by < peers]
    return lax.ppermute(value, axis, pairs)


def norm_rows(values):
    scale = lax.rsqrt(jnp.mean(values * values, axis=1, keepdims=True) + EPS)
    return (values * scale).astype(jnp.bfloat16)


def block_prior(normed, dilation_step):
    rows = normed.shape[0]
    whole = dilation_step // rows
    part = dilation_step % rows
    pieces = []
    if part > 0:
        pieces.append(from_behind(normed[rows - part :], ("seqa", "seqb"), whole + 1))
    head = normed[: rows - part]
    if whole > 0:
        head = from_behind(head, ("seqa", "seqb"), whole)
    pieces.append(head)
    return jnp.concatenate(pieces, axis=0)


def one_layer(hidden_state, tap_prev, tap_now, bias, mixing, dilation_step):
    normed = norm_rows(hidden_state)
    earlier = block_prior(normed, dilation_step)
    dim = hidden_state.shape[1]
    pre = bias[None, :] + jnp.dot(
        earlier,
        lax.all_gather(tap_prev, "seqa", axis=0, tiled=True),
        preferred_element_type=jnp.float32,
    )
    pre = pre + jnp.dot(
        normed,
        lax.all_gather(tap_now, "seqa", axis=0, tiled=True),
        preferred_element_type=jnp.float32,
    )
    hidden = (pre[:, :dim] * jax.nn.sigmoid(pre[:, dim:])).astype(jnp.bfloat16)
    return hidden_state + jnp.dot(
        hidden,
        lax.all_gather(mixing, "seqa", axis=1, tiled=True),
        preferred_element_type=jnp.float32,
    )


def plain_local(sequence_input, w_prev, w_now, conv_bias, w_mix):
    state = sequence_input.astype(jnp.float32)
    for layer, step in enumerate(DILATIONS):
        state = one_layer(
            state, w_prev[layer], w_now[layer], conv_bias[layer], w_mix[layer], step
        )
    return state.astype(jnp.bfloat16)


def flip(value, bit):
    return value + bit - 2 * bit * ((value // bit) % 2)


def block_kernel(
    na, nb, part, edge,
    x_hbm, wp_hbm, wn_hbm, bias_ref, wm_hbm,
    out_hbm,
    w, xin, xt, xp, state1, state2, u0, h0, u1, h1, u2, h2, pre, oback, ohome,
    load_sem, x_sem, out_sem, send, recv, halo_send, halo_recv, hello,
):
    layers, dim = wp_hbm.shape[0], x_hbm.shape[1]
    wide = 2 * dim
    shard = wp_hbm.shape[1]
    rows = x_hbm.shape[0]
    n = na * nb
    tail = DILATIONS[0]
    window = edge + tail
    lead_rows = edge + part
    f32, bf16 = jnp.float32, jnp.bfloat16
    a, b = lax.axis_index("seqa"), lax.axis_index("seqb")
    me = a * nb + b
    a1, a2 = flip(a, 1), flip(a, 2)
    b1, b2 = flip(b, 1), flip(b, 2)
    tiles = shard // TILE
    zs = tiles // 5
    ys = tiles // 2 - zs
    yb, zb = b % 2, b // 2 % 2
    shares = [(ys, zs), (ys - 2, zs), (ys - 1, zs)]

    def at(index):
        return (index // nb, index % nb)

    hop = DILATIONS[2] // rows
    half, q = b // hop, b % hop
    other = 1 - half
    pair = (a, (b + hop) % nb)
    wrap = (q + 1) // hop
    next_b = half * hop + (q + 1) % hop
    last_b = half * hop + (q + hop - 1) % hop
    after_a, before_a = (a + 1) % na, (a + na - 1) % na
    up, down = a + 1 < na, a > 0
    has_next, has_last = me + 1 < n, me > 0
    has_far, had_far = me + hop < n, me >= hop
    lead = jnp.where(q == 0, other, half)

    def place1(s):
        return pl.multiple_of(jnp.where(s == lead, 0, lead_rows), TILE)

    def place2(s):
        return pl.multiple_of(jnp.where(s == half, 0, lead_rows), TILE)

    loads = []
    for l in range(layers):
        loads.append([
            pltpu.make_async_copy(wp_hbm.at[l], w.at[l, a, :, pl.ds(0, wide)], load_sem.at[l, 0]),
            pltpu.make_async_copy(wn_hbm.at[l], w.at[l, a, :, pl.ds(wide, wide)], load_sem.at[l, 1]),
            pltpu.make_async_copy(wm_hbm.at[l], w.at[l, a, :, pl.ds(2 * wide, dim)], load_sem.at[l, 2]),
        ])
    for c in loads[0]:
        c.start()
    x_load = pltpu.make_async_copy(x_hbm, xin, x_sem)
    x_load.start()
    for l in range(1, layers):
        for c in loads[l]:
            c.start()

    z = b // 2
    inner = jnp.logical_and(z > 0, z < nb // 2 - 1)
    beside = (a, (b + nb - 2 + 4 * (z % 2)) % nb)

    def greet(sem, more):
        count = 4
        for dev in ((a1, b), (a2, b), (a, b1), (a, b2)):
            pl.semaphore_signal(sem, inc=1, device_id=dev, device_id_type=MESH_ID)
        for to, dev, come in [(inner, beside, inner)] + more:
            @pl.when(to)
            def _(dev=dev):
                pl.semaphore_signal(sem, inc=1, device_id=dev, device_id_type=MESH_ID)

            count = count + come.astype(jnp.int32)
        pl.semaphore_wait(sem, count)

    both = jnp.logical_and
    greet(pltpu.get_barrier_semaphore(), [
        (both(b == 0, down), (before_a, nb - 1), both(b == nb - 1, up)),
        (half == 0, pair, half == 1),
        (both(half == 0, down), (before_a, (b + hop) % nb), both(half == 1, up)),
        (q == 0, (a, last_b), wrap == 1),
        (both(q == 0, down), (before_a, last_b), both(wrap == 1, up)),
    ])

    def move(l, k, owner, start, size, dev):
        ref = w.at[l, owner, pl.ds(pl.multiple_of(start * TILE, TILE), size * TILE)]
        return pltpu.make_async_remote_copy(
            src_ref=ref, dst_ref=ref, send_sem=send.at[l, k], recv_sem=recv.at[l, k],
            device_id=dev, device_id_type=MESH_ID,
        )

    core, across, ynear, znear = (a1, b), (a2, b), (a, b1), (a, b2)
    moves, orders, lasts = [], [], []
    for l, (y, z) in enumerate(shares):
        rest = tiles - 2 * (y + z)
        own = (yb * y, 2 * y + zb * z, 2 * (y + z))
        theirs = ((1 - yb) * y, 2 * y + (1 - zb) * z)
        sizes = (y, z, rest)
        order = [(1, i) for i in range(z)] + [(0, i) for i in range(y)] + [(2, i) for i in range(rest)]
        pieces = len(order)
        here = [move(l, k, a, own[f] + i, 1, across) for k, (f, i) in enumerate(order)]
        relays = {}
        for k, (f, i) in enumerate(order):
            if f < 2:
                relays[k] = len(here)
                here.append(move(l, len(here), a2, own[f] + i, 1, (ynear, znear)[f]))
        last = len(here)
        here.append(move(l, last, a, 0, tiles, core))
        for f in range(3):
            if sizes[f]:
                here.append(move(l, len(here), a2, own[f], sizes[f], core))
        for f in range(2):
            here.append(move(l, len(here), a2, theirs[f], sizes[f], core))
        moves.append(here)
        orders.append((order, sizes, relays))
        lasts.append(last)

    def start_weights(l):
        for k in range(len(orders[l][0])):
            moves[l][k].start()
        moves[l][lasts[l]].start()

    def relay(l, k):
        order, sizes, relays = orders[l]
        moves[l][k].wait_recv()
        f, i = order[k]
        if k in relays:
            moves[l][relays[k]].start()
        if i == sizes[f] - 1:
            moves[l][lasts[l] + 1 + f].start()

    def gather(l, f):
        order, sizes, relays = orders[l]
        for k in relays:
            if order[k][0] == f:
                moves[l][relays[k]].wait_recv()
        moves[l][len(moves[l]) - 2 + f].start()

    def finish(l):
        for k in range(lasts[l], len(moves[l])):
            moves[l][k].wait_recv()

    def halo(src, dst, slot, dev):
        return pltpu.make_async_remote_copy(
            src_ref=src, dst_ref=dst, send_sem=halo_send.at[slot], recv_sem=halo_recv.at[slot],
            device_id=dev, device_id_type=MESH_ID,
        )

    mine = pl.ds(edge, part)
    x_next = halo(xin.at[pl.ds(rows - tail, tail)], xt, 0, at((me + 1) % n))
    x_pair = halo(xin.at[pl.ds(pl.multiple_of(other * edge, TILE), window)], xp, 1, pair)
    second_home = halo(u1.at[mine], h1.at[mine], 2, at((me + 1) % n))

    def second(s):
        to = s + wrap
        slot = to % 2
        return halo(
            u1.at[pl.ds(place1(s), edge)], h1.at[pl.ds(place1_at_next(slot), edge)],
            3 + slot, ((a + to // 2) % na, next_b),
        ), a + to // 2 < na

    def place1_at_next(slot):
        first = jnp.where(wrap == 1, other, half)
        return pl.multiple_of(jnp.where(slot == first, 0, lead_rows), TILE)

    third_home = halo(u2.at[mine], h2.at[mine], 5, at((me + hop) % n))
    third = halo(u2.at[pl.ds(place2(1), edge)], h2.at[pl.ds(place2(0), edge)], 6, (after_a, b))
    edge_rows = pl.ds(pl.multiple_of(part + half * edge, TILE), edge)
    back = halo(oback, out_hbm.at[edge_rows], 7, pair)
    near_cut = (b // 2) % 2 != half

    for c in loads[0]:
        c.wait()
    start_weights(0)
    x_load.wait()
    greet(hello, [])
    pl.when(has_next)(x_next.start)
    pl.when(near_cut)(x_pair.start)
    for l in range(1, layers):
        for c in loads[l]:
            c.wait()
        start_weights(l)

    @pl.when(me == 0)
    def _():
        xt[...] = jnp.zeros(xt.shape, xt.dtype)
        h1[mine] = jnp.zeros((part, dim), h1.dtype)

    @pl.when(both(a == 0, q == 0))
    def _():
        h1[pl.ds(place1(0), edge)] = jnp.zeros((edge, dim), h1.dtype)

    @pl.when(a == 0)
    def _():
        h2[pl.ds(place2(0), edge)] = jnp.zeros((edge, dim), h2.dtype)

    @pl.when(jnp.logical_not(had_far))
    def _():
        h2[mine] = jnp.zeros((part, dim), h2.dtype)

    def enter(ref, start, lo):
        normed = norm_rows(ref[pl.ds(start, window)].astype(f32))
        h0[lo : lo + edge] = normed[:edge]
        u0[lo : lo + edge] = normed[tail:]

    def tap(l, lo):
        return w[l, :, :, lo : lo + wide].reshape(na * shard, wide)

    front, rear = (0, lead_rows), (lead_rows, edge)

    def now_part(l, now, span):
        lo, size = span
        pre[lo : lo + size] = bias_ref[l : l + 1, :] + jnp.dot(
            now[lo : lo + size], tap(l, wide), preferred_element_type=f32
        )

    def rest_part(l, earlier, span):
        lo, size = span
        total = pre[lo : lo + size] + jnp.dot(
            earlier[lo : lo + size], tap(l, 0), preferred_element_type=f32
        )
        hidden = (total[:, :dim] * jax.nn.sigmoid(total[:, dim:])).astype(bf16)
        mix = w[l, :, :, 2 * wide :].reshape(na * shard, dim)
        return lax.dot_general(hidden, mix, (((1,), (1,)), ((), ())), preferred_element_type=f32)

    enter(xin, pl.multiple_of(half * edge, TILE), 0)
    u0[mine] = norm_rows(xin[:part].astype(f32))
    relay(0, 0)
    relay(0, 1)
    pl.when(jnp.logical_not(near_cut))(x_pair.start)
    for k in range(2, len(orders[0][0])):
        relay(0, k)
    gather(0, 1)
    relay(1, 0)
    gather(0, 0)
    pl.when(has_last)(x_next.wait_recv)
    h0[mine] = norm_rows(xt[...].astype(f32))
    relay(1, 1)
    finish(0)

    def leave1(new, spot):
        state1[spot] = new
        u1[spot] = norm_rows(new)

    now_part(0, u0, front)
    relay(1, 2)
    grown = rest_part(0, h0, front)
    own_start = pl.multiple_of(tail + half * edge, TILE)
    leave1(xin[pl.ds(own_start, edge)].astype(f32) + grown[:edge], pl.ds(place1(half), edge))
    copy, there = second(half)
    pl.when(there)(copy.start)
    leave1(xin[:part].astype(f32) + grown[edge:], mine)
    pl.when(has_next)(second_home.start)
    x_pair.wait_recv()
    enter(xp, 0, lead_rows)
    now_part(0, u0, rear)
    relay(1, 3)
    grown = rest_part(0, h0, rear)
    leave1(xp[tail:].astype(f32) + grown, pl.ds(place1(other), edge))
    copy, there = second(other)
    pl.when(there)(copy.start)
    for k in range(4, len(orders[1][0])):
        relay(1, k)
    gather(1, 1)
    gather(1, 0)
    finish(1)
    now_part(1, u1, front)
    now_part(1, u1, rear)
    relay(2, 0)

    def takes(s):
        @pl.when(jnp.logical_or(q + s > 0, down))
        def _():
            spot = pl.ds(place1(s), edge)
            halo(u1.at[spot], h1.at[spot], 3 + s, pair).wait_recv()

    def leave2(new, spot):
        normed = norm_rows(new)
        state2[spot] = new
        u2[spot] = normed
        return normed

    def leave2_edge(new, s):
        normed = leave2(new, pl.ds(place2(s), edge))

        @pl.when(s == 0)
        def _():
            h2[pl.ds(place2(1), edge)] = normed

        @pl.when(both(s == 1, up))
        def _():
            third.start()

    takes(lead)
    pl.when(has_last)(second_home.wait_recv)
    new = state1[:lead_rows] + rest_part(1, h1, front)
    leave2(new[edge:], mine)
    pl.when(has_far)(third_home.start)
    leave2_edge(new[:edge], lead)
    relay(2, 1)
    relay(2, 2)
    takes(1 - lead)
    leave2_edge(state1[lead_rows:] + rest_part(1, h1, rear), 1 - lead)
    for k in range(3, len(orders[2][0])):
        relay(2, k)
    gather(2, 1)
    gather(2, 0)
    finish(2)

    def takes_third(s):
        @pl.when(both(s == 0, down))
        def _():
            third.wait_recv()

    now_part(2, u2, rear)
    takes_third(other)
    oback[...] = (state2[lead_rows:] + rest_part(2, h2, rear)).astype(bf16)
    back.start()
    now_part(2, u2, front)
    takes_third(half)
    pl.when(had_far)(third_home.wait_recv)
    ohome[...] = (state2[:lead_rows] + rest_part(2, h2, front)).astype(bf16)
    outs = [
        pltpu.make_async_copy(ohome.at[pl.ds(0, edge)], out_hbm.at[edge_rows], out_sem.at[0]),
        pltpu.make_async_copy(ohome.at[mine], out_hbm.at[pl.ds(0, part)], out_sem.at[1]),
    ]
    for c in outs:
        c.start()
    for l in range(layers):
        for m in moves[l]:
            m.wait_send()
    for s in range(2):
        copy, there = second(s)
        pl.when(there)(copy.wait_send)
    pl.when(has_next)(second_home.wait_send)
    pl.when(has_next)(x_next.wait_send)
    pl.when(has_far)(third_home.wait_send)
    pl.when(up)(third.wait_send)
    x_pair.wait_send()
    for c in outs:
        c.wait()
    back.wait_send()
    back.wait_recv()


def kernel_local(na, nb, sequence_input, w_prev, w_now, conv_bias, w_mix):
    rows, dim = sequence_input.shape
    layers, shard, wide = w_prev.shape
    tail = DILATIONS[0]
    part = tail
    edge = (rows - part) // 2
    bf16, f32 = jnp.bfloat16, jnp.float32
    halos, copies = 8, shard // TILE + 6
    anywhere = pl.BlockSpec(memory_space=pl.ANY)
    vmem = pl.BlockSpec(memory_space=pltpu.VMEM)
    block = (rows, dim)
    return pl.pallas_call(
        functools.partial(block_kernel, na, nb, part, edge),
        out_shape=jax.ShapeDtypeStruct((rows, dim), bf16),
        in_specs=[anywhere, anywhere, anywhere, vmem, anywhere],
        out_specs=anywhere,
        scratch_shapes=[
            pltpu.VMEM((layers, na, shard, 2 * wide + dim), bf16),
            pltpu.VMEM(block, bf16),
            pltpu.VMEM((tail, dim), bf16),
            pltpu.VMEM((edge + tail, dim), bf16),
            pltpu.VMEM(block, f32),
            pltpu.VMEM(block, f32),
            pltpu.VMEM(block, bf16),
            pltpu.VMEM(block, bf16),
            pltpu.VMEM(block, bf16),
            pltpu.VMEM(block, bf16),
            pltpu.VMEM(block, bf16),
            pltpu.VMEM(block, bf16),
            pltpu.VMEM((rows, wide), f32),
            pltpu.VMEM((edge, dim), bf16),
            pltpu.VMEM((edge + part, dim), bf16),
            pltpu.SemaphoreType.DMA((layers, 3)),
            pltpu.SemaphoreType.DMA,
            pltpu.SemaphoreType.DMA((2,)),
            pltpu.SemaphoreType.DMA((layers, copies)),
            pltpu.SemaphoreType.DMA((layers, copies)),
            pltpu.SemaphoreType.DMA((halos,)),
            pltpu.SemaphoreType.DMA((halos,)),
            pltpu.SemaphoreType.REGULAR,
        ],
        compiler_params=pltpu.CompilerParams(
            collective_id=0, has_side_effects=True, vmem_limit_bytes=56 * 2**20
        ),
    )(sequence_input, w_prev, w_now, conv_bias, jnp.swapaxes(w_mix, 1, 2))


def local(na, nb, sequence_input, w_prev, w_now, conv_bias, w_mix):
    rows = sequence_input.shape[0]
    shard = w_prev.shape[1]
    fits = (
        na == 4
        and nb % GROUP == 0
        and shard % TILE == 0
        and shard % (2 * TILE) == 0
        and shard >= 5 * TILE
        and rows % (4 * TILE) == 0
        and rows == 4 * DILATIONS[0]
        and DILATIONS[1] == rows
        and 2 * DILATIONS[2] == nb * rows
    )
    body = functools.partial(kernel_local, na, nb) if fits else plain_local
    return body(sequence_input, w_prev, w_now, conv_bias, w_mix)


def solution(mesh):
    return jax.shard_map(
        functools.partial(local, mesh.shape["seqa"], mesh.shape["seqb"]),
        mesh=mesh,
        in_specs=(
            P(("seqa", "seqb"), None),
            P(None, "seqa", None),
            P(None, "seqa", None),
            P(),
            P(None, None, "seqa"),
        ),
        out_specs=P(("seqa", "seqb"), None),
        check_vma=False,
    )
```

time: 73.2 us -> 69.2 us (0.945)
  the two profiles are of different devices: /device:TPU:29 before, /device:TPU:5 now
where the time goes in v2:
time: 69.2 us; the launch traced here: 69 us
  Pallas kernels  67 us (97%)
  local copies, waits for them, and re-layouts  1.98 us (3%)
    pallas_call x1, Pallas kernels, kernel_local(): pl.pallas_call(functools.partial(block_kernel, na, nb, part, edge), out_s...  67 us
    unnamed x1, local copies, waits for them, and re-layouts  1.98 us

profile of v2, /device:TPU:5, one launch (start us, length us, event | category | flops | bytes accessed | tf_op | source)
XLA Modules:
  0.0 69.0 jit_solution(15043503948512363322)
XLA Ops:
  0.0 67.0 %shard_map.55 = bf16[512,640]{1,0:T(8,128)(2,1)} custom-call(bf16[512,640]{1,0:T(8,128)(2,1)} %x_hbm.1, bf16[3,160,1280]{2,1,0:T(8,128)(2,1)} %wp_hbm.1, bf16[3,160,1280]{2,1,0:T(8,128)(2,1)} %wn_hbm.1, f32[3,1280]{1,0:T(4,128)} %bias_ref.1, bf16[3,160,640]{2,1,0:T(8,128)(2,1)} %bitcast.1), custom_call_target="tpu_custom_call" | custom-call | tf_op jit(solution)/shard_map/pallas_call | solution.py:437
  67.0 2.0 %copy.7 = bf16[512,640]{1,0:T(8,128)(2,1)} copy(bf16[512,640]{1,0:T(8,128)(2,1)} %shard_map.55) | data formatting | bytes 1310720

commit v3 on v2

--- a/solution.py
+++ b/solution.py
@@ -77,9 +77,9 @@
 def block_kernel(
     na, nb, part, edge,
     x_hbm, wp_hbm, wn_hbm, bias_ref, wm_hbm,
-    out_hbm,
-    w, xin, xt, xp, state1, state2, u0, h0, u1, h1, u2, h2, pre, oback, ohome,
-    load_sem, x_sem, out_sem, send, recv, halo_send, halo_recv, hello,
+    out_ref,
+    w, xin, xt, xp, state1, state2, u0, h0, u1, h1, u2, h2, pre, oback,
+    load_sem, x_sem, send, recv, halo_send, halo_recv, hello,
 ):
     layers, dim = wp_hbm.shape[0], x_hbm.shape[1]
     wide = 2 * dim
@@ -98,7 +98,7 @@
     zs = tiles // 5
     ys = tiles // 2 - zs
     yb, zb = b % 2, b // 2 % 2
-    shares = [(ys, zs), (ys - 2, zs), (ys - 1, zs)]
+    shares = [(ys, zs), (ys - 2, zs), (ys - 1, zs - 1)]
 
     def at(index):
         return (index // nb, index % nb)
@@ -228,7 +228,7 @@
 
     mine = pl.ds(edge, part)
     x_next = halo(xin.at[pl.ds(rows - tail, tail)], xt, 0, at((me + 1) % n))
-    x_pair = halo(xin.at[pl.ds(pl.multiple_of(other * edge, TILE), window)], xp, 1, pair)
+    x_pair = halo(xin.at[pl.ds(pl.multiple_of(part - tail + other * edge, TILE), window)], xp, 1, pair)
     second_home = halo(u1.at[mine], h1.at[mine], 2, at((me + 1) % n))
 
     def second(s):
@@ -246,7 +246,7 @@
     third_home = halo(u2.at[mine], h2.at[mine], 5, at((me + hop) % n))
     third = halo(u2.at[pl.ds(place2(1), edge)], h2.at[pl.ds(place2(0), edge)], 6, (after_a, b))
     edge_rows = pl.ds(pl.multiple_of(part + half * edge, TILE), edge)
-    back = halo(oback, out_hbm.at[edge_rows], 7, pair)
+    back = halo(oback, out_ref.at[edge_rows], 7, pair)
     near_cut = (b // 2) % 2 != half
 
     for c in loads[0]:
@@ -303,8 +303,11 @@
         mix = w[l, :, :, 2 * wide :].reshape(na * shard, dim)
         return lax.dot_general(hidden, mix, (((1,), (1,)), ((), ())), preferred_element_type=f32)
 
-    enter(xin, pl.multiple_of(half * edge, TILE), 0)
-    u0[mine] = norm_rows(xin[:part].astype(f32))
+    enter(xin, pl.multiple_of(part - tail + half * edge, TILE), 0)
+    home = norm_rows(xin[:part].astype(f32))
+    u0[mine] = home
+    if part > tail:
+        h0[edge + tail : lead_rows] = home[: part - tail]
     relay(0, 0)
     relay(0, 1)
     pl.when(jnp.logical_not(near_cut))(x_pair.start)
@@ -314,7 +317,7 @@
     relay(1, 0)
     gather(0, 0)
     pl.when(has_last)(x_next.wait_recv)
-    h0[mine] = norm_rows(xt[...].astype(f32))
+    h0[edge : edge + tail] = norm_rows(xt[...].astype(f32))
     relay(1, 1)
     finish(0)
 
@@ -325,12 +328,12 @@
     now_part(0, u0, front)
     relay(1, 2)
     grown = rest_part(0, h0, front)
-    own_start = pl.multiple_of(tail + half * edge, TILE)
+    own_start = pl.multiple_of(part + half * edge, TILE)
     leave1(xin[pl.ds(own_start, edge)].astype(f32) + grown[:edge], pl.ds(place1(half), edge))
+    leave1(xin[:part].astype(f32) + grown[edge:], mine)
+    pl.when(has_next)(second_home.start)
     copy, there = second(half)
     pl.when(there)(copy.start)
-    leave1(xin[:part].astype(f32) + grown[edge:], mine)
-    pl.when(has_next)(second_home.start)
     x_pair.wait_recv()
     enter(xp, 0, lead_rows)
     now_part(0, u0, rear)
@@ -379,9 +382,10 @@
     leave2_edge(new[:edge], lead)
     relay(2, 1)
     relay(2, 2)
+    relay(2, 3)
     takes(1 - lead)
     leave2_edge(state1[lead_rows:] + rest_part(1, h1, rear), 1 - lead)
-    for k in range(3, len(orders[2][0])):
+    for k in range(4, len(orders[2][0])):
         relay(2, k)
     gather(2, 1)
     gather(2, 0)
@@ -399,13 +403,9 @@
     now_part(2, u2, front)
     takes_third(half)
     pl.when(had_far)(third_home.wait_recv)
-    ohome[...] = (state2[:lead_rows] + rest_part(2, h2, front)).astype(bf16)
-    outs = [
-        pltpu.make_async_copy(ohome.at[pl.ds(0, edge)], out_hbm.at[edge_rows], out_sem.at[0]),
-        pltpu.make_async_copy(ohome.at[mine], out_hbm.at[pl.ds(0, part)], out_sem.at[1]),
-    ]
-    for c in outs:
-        c.start()
+    new = (state2[:lead_rows] + rest_part(2, h2, front)).astype(bf16)
+    out_ref[edge_rows] = new[:edge]
+    out_ref[:part] = new[edge:]
     for l in range(layers):
         for m in moves[l]:
             m.wait_send()
@@ -417,8 +417,6 @@
     pl.when(has_far)(third_home.wait_send)
     pl.when(up)(third.wait_send)
     x_pair.wait_send()
-    for c in outs:
-        c.wait()
     back.wait_send()
     back.wait_recv()
 
@@ -427,7 +425,7 @@
     rows, dim = sequence_input.shape
     layers, shard, wide = w_prev.shape
     tail = DILATIONS[0]
-    part = tail
+    part = 3 * tail // 2
     edge = (rows - part) // 2
     bf16, f32 = jnp.bfloat16, jnp.float32
     halos, copies = 8, shard // TILE + 6
@@ -436,9 +434,9 @@
     block = (rows, dim)
     return pl.pallas_call(
         functools.partial(block_kernel, na, nb, part, edge),
-        out_shape=jax.ShapeDtypeStruct((rows, dim), bf16),
+        out_shape=pltpu.VMEM((rows, dim), bf16),
         in_specs=[anywhere, anywhere, anywhere, vmem, anywhere],
-        out_specs=anywhere,
+        out_specs=vmem,
         scratch_shapes=[
             pltpu.VMEM((layers, na, shard, 2 * wide + dim), bf16),
             pltpu.VMEM(block, bf16),
@@ -454,10 +452,8 @@
             pltpu.VMEM(block, bf16),
             pltpu.VMEM((rows, wide), f32),
             pltpu.VMEM((edge, dim), bf16),
-            pltpu.VMEM((edge + part, dim), bf16),
             pltpu.SemaphoreType.DMA((layers, 3)),
             pltpu.SemaphoreType.DMA,
-            pltpu.SemaphoreType.DMA((2,)),
             pltpu.SemaphoreType.DMA((layers, copies)),
             pltpu.SemaphoreType.DMA((layers, copies)),
             pltpu.SemaphoreType.DMA((halos,)),

time: 69.2 us -> 65 us (0.939)
  the two profiles are of different devices: /device:TPU:5 before, /device:TPU:23 now
where the time goes in v3:
time: 65 us; the launch traced here: 64.9 us
  Pallas kernels  64 us (98%)
  local copies, waits for them, and re-layouts  0.84 us (1%)
    pallas_call x1, Pallas kernels, kernel_local(): pl.pallas_call(functools.partial(block_kernel, na, nb, part, edge), out_s...  64 us

profile of v3, /device:TPU:23, one launch (start us, length us, event | category | flops | bytes accessed | tf_op | source)
XLA Modules:
  0.0 64.9 jit_solution(4236397313361844800)
XLA Ops:
  0.0 64.0 %shard_map.55 = bf16[512,640]{1,0:T(8,128)(2,1)S(1)} custom-call(bf16[512,640]{1,0:T(8,128)(2,1)} %x_hbm.1, bf16[3,160,1280]{2,1,0:T(8,128)(2,1)} %wp_hbm.1, bf16[3,160,1280]{2,1,0:T(8,128)(2,1)} %wn_hbm.1, f32[3,1280]{1,0:T(4,128)} %bias_ref.1, bf16[3,160,640]{2,1,0:T(8,128)(2,1)} %bitcast.1), custom_call_target="tpu_custom_call" | custom-call | tf_op jit(solution)/shard_map/pallas_call | solution.py:435
  64.0 0.8 %copy.7 = bf16[512,640]{1,0:T(8,128)(2,1)} copy(bf16[512,640]{1,0:T(8,128)(2,1)S(1)} %shard_map.55) | data formatting | bytes 1310720

commit v4 on v3

--- a/solution.py
+++ b/solution.py
@@ -98,7 +98,7 @@
     zs = tiles // 5
     ys = tiles // 2 - zs
     yb, zb = b % 2, b // 2 % 2
-    shares = [(ys, zs), (ys - 2, zs), (ys - 1, zs - 1)]
+    shares = [(ys, zs, None), (ys - 2, zs, None), (ys - 1, zs - 1, None)]
 
     def at(index):
         return (index // nb, index % nb)
@@ -170,51 +170,128 @@
         )
 
     core, across, ynear, znear = (a1, b), (a2, b), (a, b1), (a, b2)
-    moves, orders, lasts = [], [], []
-    for l, (y, z) in enumerate(shares):
-        rest = tiles - 2 * (y + z)
-        own = (yb * y, 2 * y + zb * z, 2 * (y + z))
+    moves, orders, lasts, sent = [], [], [], []
+    fours, rest4 = tiles // 5, tiles - tiles // 5 * 4
+    p = b % GROUP
+    py, pz = flip(p, 1), flip(p, 2)
+    pyz = flip(py, 2)
+    plan = [(across, p, i) for i in range(fours)] + [(across, GROUP, i) for i in range(rest4)]
+    plan += [(ynear, p, i) for i in range(fours)] + [(znear, p, i) for i in range(fours)]
+    plan += [(ynear, pz, i) for i in range(fours)]
+    x_own, x_rest, y_own, z_own, y_hop, plain = (
+        0, fours, fours + rest4, 2 * fours + rest4, 3 * fours + rest4, 4 * fours + rest4
+    )
+    here = [
+        move(0, k, a if dev is across else a2, block * fours + i, 1, dev)
+        for k, (dev, block, i) in enumerate(plan)
+    ]
+    here.append(move(0, plain, a, 0, tiles, core))
+    for k, (block, size) in enumerate(
+        [(p, fours), (GROUP, rest4), (py, fours), (pz, fours), (pyz, fours)]
+    ):
+        here.append(move(0, plain + 1 + k, a2, block * fours, size, core))
+    moves.append(here)
+    sent += [(m, None) for m in here]
+    orders.append(([(2, 0)] * (fours + rest4), None, None, None, None, None))
+    lasts.append(plain)
+
+    def arrive(k, then=()):
+        moves[0][k].wait_recv()
+        for t in then:
+            moves[0][t].start()
+
+    def layer0_own():
+        for i in range(fours):
+            arrive(x_own + i, (y_own + i, z_own + i))
+        moves[0][plain + 1].start()
+
+    def layer0_rest():
+        for i in range(max(fours, rest4)):
+            if i < rest4:
+                arrive(x_rest + i)
+            if i < fours:
+                arrive(z_own + i, (y_hop + i,))
+        moves[0][plain + 2].start()
+        moves[0][plain + 4].start()
+        for i in range(fours):
+            arrive(y_own + i)
+        moves[0][plain + 3].start()
+
+    def layer0_hops():
+        for i in range(fours):
+            arrive(y_hop + i)
+        moves[0][plain + 5].start()
+
+    for l, (y, z, spread) in enumerate(shares[1:], 1):
+        pick = 0 if spread is None else 1
+        rest = tiles - 2 * (y + z + pick)
+        swap = 2 * (y + z)
+        own = (yb * y, 2 * y + zb * z, swap + 2 * pick, swap + zb, swap + 1 - zb)
         theirs = ((1 - yb) * y, 2 * y + (1 - zb) * z)
-        sizes = (y, z, rest)
-        order = [(1, i) for i in range(z)] + [(0, i) for i in range(y)] + [(2, i) for i in range(rest)]
-        pieces = len(order)
-        here = [move(l, k, a, own[f] + i, 1, across) for k, (f, i) in enumerate(order)]
+        sizes = (y, z, rest, pick, pick)
+        order = [(1, i) for i in range(z)] + [(3, i) for i in range(pick)]
+        order += [(0, i) for i in range(y)] + [(2, i) for i in range(rest)] + [(4, i) for i in range(pick)]
+        mine = spread and spread(a // 2, yb)
+        away = spread and jnp.logical_not(spread(1 - a // 2, yb))
+        here = [(move(l, k, a, own[f] + i, 1, across), away if f == 4 else None) for k, (f, i) in enumerate(order)]
         relays = {}
         for k, (f, i) in enumerate(order):
-            if f < 2:
+            if f in (0, 1, 3):
                 relays[k] = len(here)
-                here.append(move(l, len(here), a2, own[f] + i, 1, (ynear, znear)[f]))
+                here.append((
+                    move(l, len(here), a2, own[f] + i, 1, znear if f else ynear), mine if f == 3 else None
+                ))
         last = len(here)
-        here.append(move(l, last, a, 0, tiles, core))
-        for f in range(3):
+        here.append((move(l, last, a, 0, tiles, core), None))
+        local = {}
+        for f in range(5):
             if sizes[f]:
-                here.append(move(l, len(here), a2, own[f], sizes[f], core))
+                local[f] = len(here)
+                here.append((move(l, len(here), a2, own[f], sizes[f], core), None))
         for f in range(2):
-            here.append(move(l, len(here), a2, theirs[f], sizes[f], core))
-        moves.append(here)
-        orders.append((order, sizes, relays))
+            here.append((move(l, len(here), a2, theirs[f], sizes[f], core), None))
+        moves.append([m for m, _ in here])
+        sent += here
+        orders.append((order, sizes, relays, local, mine, away))
         lasts.append(last)
 
+    def maybe(there, do):
+        if there is None:
+            do()
+        else:
+            pl.when(there)(do)
+
     def start_weights(l):
-        for k in range(len(orders[l][0])):
-            moves[l][k].start()
+        order, away = orders[l][0], orders[l][5]
+        for k, (f, _) in enumerate(order):
+            maybe(away if f == 4 else None, moves[l][k].start)
         moves[l][lasts[l]].start()
 
     def relay(l, k):
-        order, sizes, relays = orders[l]
-        moves[l][k].wait_recv()
+        order, sizes, relays, local, mine, _ = orders[l]
         f, i = order[k]
-        if k in relays:
-            moves[l][relays[k]].start()
-        if i == sizes[f] - 1:
-            moves[l][lasts[l] + 1 + f].start()
+
+        def here():
+            moves[l][k].wait_recv()
+            if k in relays:
+                maybe(mine if f == 3 else None, moves[l][relays[k]].start)
+            if i == sizes[f] - 1:
+                moves[l][local[f]].start()
+
+        maybe(jnp.logical_not(mine) if f == 4 else None, here)
 
     def gather(l, f):
-        order, sizes, relays = orders[l]
+        order, sizes, relays, local, mine, _ = orders[l]
         for k in relays:
             if order[k][0] == f:
                 moves[l][relays[k]].wait_recv()
         moves[l][len(moves[l]) - 2 + f].start()
+        for k in relays:
+            if f == 1 and order[k][0] == 3:
+                @pl.when(mine)
+                def _(k=k):
+                    moves[l][relays[k]].wait_recv()
+                    moves[l][local[4]].start()
 
     def finish(l):
         for k in range(lasts[l], len(moves[l])):
@@ -228,7 +305,14 @@
 
     mine = pl.ds(edge, part)
     x_next = halo(xin.at[pl.ds(rows - tail, tail)], xt, 0, at((me + 1) % n))
-    x_pair = halo(xin.at[pl.ds(pl.multiple_of(part - tail + other * edge, TILE), window)], xp, 1, pair)
+    cut = window // TILE // 2 * TILE
+    x_pair = [
+        halo(
+            xin.at[pl.ds(pl.multiple_of(part - tail + other * edge + lo, TILE), size)],
+            xp.at[pl.ds(lo, size)], slot, pair,
+        )
+        for lo, size, slot in ((0, cut, 1), (cut, window - cut, 8))
+    ]
     second_home = halo(u1.at[mine], h1.at[mine], 2, at((me + 1) % n))
 
     def second(s):
@@ -255,7 +339,13 @@
     x_load.wait()
     greet(hello, [])
     pl.when(has_next)(x_next.start)
-    pl.when(near_cut)(x_pair.start)
+
+    def pair_rest():
+        pl.when(jnp.logical_not(near_cut))(x_pair[0].start)
+        pl.when(jnp.logical_not(near_cut))(x_pair[1].start)
+
+    pl.when(near_cut)(x_pair[0].start)
+    pl.when(near_cut)(x_pair[1].start)
     for l in range(1, layers):
         for c in loads[l]:
             c.wait()
@@ -308,14 +398,11 @@
     u0[mine] = home
     if part > tail:
         h0[edge + tail : lead_rows] = home[: part - tail]
-    relay(0, 0)
-    relay(0, 1)
-    pl.when(jnp.logical_not(near_cut))(x_pair.start)
-    for k in range(2, len(orders[0][0])):
-        relay(0, k)
-    gather(0, 1)
+    layer0_own()
+    pair_rest()
+    layer0_rest()
     relay(1, 0)
-    gather(0, 0)
+    layer0_hops()
     pl.when(has_last)(x_next.wait_recv)
     h0[edge : edge + tail] = norm_rows(xt[...].astype(f32))
     relay(1, 1)
@@ -334,7 +421,8 @@
     pl.when(has_next)(second_home.start)
     copy, there = second(half)
     pl.when(there)(copy.start)
-    x_pair.wait_recv()
+    for c in x_pair:
+        c.wait_recv()
     enter(xp, 0, lead_rows)
     now_part(0, u0, rear)
     relay(1, 3)
@@ -374,21 +462,31 @@
         def _():
             third.start()
 
+    relay(2, 1)
+    def middle():
+        relay(2, 2)
+
+    pl.when(b % 2 == 0)(middle)
     takes(lead)
     pl.when(has_last)(second_home.wait_recv)
     new = state1[:lead_rows] + rest_part(1, h1, front)
     leave2(new[edge:], mine)
     pl.when(has_far)(third_home.start)
     leave2_edge(new[:edge], lead)
-    relay(2, 1)
-    relay(2, 2)
+    pl.when(jnp.logical_not(b % 2 == 0))(middle)
     relay(2, 3)
+
+    def last_relays():
+        for k in range(4, len(orders[2][0])):
+            relay(2, k)
+        gather(2, 1)
+        gather(2, 0)
+
+    pl.when(q == 0)(last_relays)
+
     takes(1 - lead)
     leave2_edge(state1[lead_rows:] + rest_part(1, h1, rear), 1 - lead)
-    for k in range(4, len(orders[2][0])):
-        relay(2, k)
-    gather(2, 1)
-    gather(2, 0)
+    pl.when(q > 0)(last_relays)
     finish(2)
 
     def takes_third(s):
@@ -396,19 +494,26 @@
         def _():
             third.wait_recv()
 
-    now_part(2, u2, rear)
-    takes_third(other)
-    oback[...] = (state2[lead_rows:] + rest_part(2, h2, rear)).astype(bf16)
-    back.start()
-    now_part(2, u2, front)
-    takes_third(half)
-    pl.when(had_far)(third_home.wait_recv)
-    new = (state2[:lead_rows] + rest_part(2, h2, front)).astype(bf16)
-    out_ref[edge_rows] = new[:edge]
-    out_ref[:part] = new[edge:]
-    for l in range(layers):
-        for m in moves[l]:
-            m.wait_send()
+    def end_rear():
+        now_part(2, u2, rear)
+        takes_third(other)
+        oback[...] = (state2[lead_rows:] + rest_part(2, h2, rear)).astype(bf16)
+        back.start()
+
+    def end_front():
+        now_part(2, u2, front)
+        takes_third(half)
+        pl.when(had_far)(third_home.wait_recv)
+        new = (state2[:lead_rows] + rest_part(2, h2, front)).astype(bf16)
+        out_ref[edge_rows] = new[:edge]
+        out_ref[:part] = new[edge:]
+
+    early = jnp.logical_or(near_cut, both(half == 0, a >= na // 2) | both(half == 1, a >= na // 2))
+    pl.when(early)(end_rear)
+    end_front()
+    pl.when(jnp.logical_not(early))(end_rear)
+    for m, there in sent:
+        maybe(there, m.wait_send)
     for s in range(2):
         copy, there = second(s)
         pl.when(there)(copy.wait_send)
@@ -416,7 +521,8 @@
     pl.when(has_next)(x_next.wait_send)
     pl.when(has_far)(third_home.wait_send)
     pl.when(up)(third.wait_send)
-    x_pair.wait_send()
+    for c in x_pair:
+        c.wait_send()
     back.wait_send()
     back.wait_recv()
 
@@ -428,7 +534,7 @@
     part = 3 * tail // 2
     edge = (rows - part) // 2
     bf16, f32 = jnp.bfloat16, jnp.float32
-    halos, copies = 8, shard // TILE + 6
+    halos, copies = 9, 2 * (shard // TILE)
     anywhere = pl.BlockSpec(memory_space=pl.ANY)
     vmem = pl.BlockSpec(memory_space=pltpu.VMEM)
     block = (rows, dim)

time: 65 us -> 64.4 us (level)
  the two profiles are of different devices: /device:TPU:23 before, /device:TPU:27 now
where the time goes in v4:
time: 64.4 us; the launch traced here: 64.2 us
  Pallas kernels  63.3 us (98%)
  local copies, waits for them, and re-layouts  0.84 us (1%)
    pallas_call x1, Pallas kernels, kernel_local(): pl.pallas_call(functools.partial(block_kernel, na, nb, part, edge), out_s...  63.3 us

profile of v4, /device:TPU:27, one launch (start us, length us, event | category | flops | bytes accessed | tf_op | source)
XLA Modules:
  0.0 64.2 jit_solution(16783358751079308543)
XLA Ops:
  0.0 63.3 %shard_map.55 = bf16[512,640]{1,0:T(8,128)(2,1)S(1)} custom-call(bf16[512,640]{1,0:T(8,128)(2,1)} %x_hbm.1, bf16[3,160,1280]{2,1,0:T(8,128)(2,1)} %wp_hbm.1, bf16[3,160,1280]{2,1,0:T(8,128)(2,1)} %wn_hbm.1, f32[3,1280]{1,0:T(4,128)} %bias_ref.1, bf16[3,160,640]{2,1,0:T(8,128)(2,1)} %bitcast.1), custom_call_target="tpu_custom_call" | custom-call | tf_op jit(solution)/shard_map/pallas_call | solution.py:541
  63.4 0.8 %copy.7 = bf16[512,640]{1,0:T(8,128)(2,1)} copy(bf16[512,640]{1,0:T(8,128)(2,1)S(1)} %shard_map.55) | data formatting | bytes 1310720
